TPU v7x, 32 devices: a whole 2x2x4 slice. The times are simulated.
32 devices in a mesh: groups: 1, fac: 32 (over z, y, x, core).
Axes of the slice: x: 2, y: 2, z: 4, core: 2. Of those that a mesh axis runs over, the one named last changes fastest.
Arguments:
- sky_image: float32 [64, 96, 4096], P(('groups', 'fac')), may hold values from 0 to 18, as said below
- measured_real: float32 [64, 96, 4096], P(('groups', 'fac')), may hold values from -6 to 6
- measured_imaginary: float32 [64, 96, 4096], P(('groups', 'fac')), may hold values from -6 to 6
- sampling_mask: int32 [64, 96, 4096], P(('groups', 'fac')), may hold values 0 or 1
- dual_field: float32 [64, 96, 4096], P('groups', None, 'fac'), may hold values from -6 to 6
Outputs:
- next_image: float32 [64, 96, 4096], P(('groups', 'fac'))
- next_dual: float32 [64, 96, 4096], P('groups', None, 'fac')
Inputs may be any that keep to these rules, and one draw needn't show every extreme that they name: `sky_image`: non-negative sky brightness.
All inputs are finite; a program needn't handle non-finite values. No bound on the sum of `sampling_mask` on one device may be relied on, other than what follows from the above.
Results may differ from a plain program's by a relative error of at most 0.00012.
Values sent between devices are 32-bit elements; how exact they have to be, the bound alone decides.
No kernel may reach another device: no remote copies, remote signals or barrier semaphores. Data moves between devices by JAX's collectives and lax.ppermute only.
A program may use at most 192 MiB of HBM per device.

v0:
```python
import jax
import jax.numpy as jnp
import numpy as np
from jax import lax
from jax.sharding import PartitionSpec as P

LEVELS = 4
low_pass = (
    0.2303778133088964,
    0.7148465705529155,
    0.6308807679298587,
    -0.0279837694168599,
    -0.1870348117190931,
    0.0308413818355607,
    0.0328830116668852,
    -0.010597401785069,
)
high_pass = tuple(((-1) ** tap_index * low_pass[7 - tap_index] for tap_index in range(8)))
primal_step = 0.6
dual_step = 0.8
ball_radius = 12.0
precise = lax.Precision.HIGHEST


def contract(pattern, left_side, right_side):
    return jnp.einsum(
        pattern, left_side, right_side, precision=precise, preferred_element_type=jnp.float32
    )


def fourier_table(length, direction):
    sample_grid = np.arange(length)
    angles = 2.0 * np.pi * (np.outer(sample_grid, sample_grid) % length) / length
    factor = 1.0 / np.sqrt(length)
    return (
        jnp.asarray(np.cos(angles) * factor, jnp.float32),
        jnp.asarray(direction * np.sin(angles) * factor, jnp.float32),
    )


def twist_table(inner_size, outer_size, length, direction):
    angles = (
        2.0
        * np.pi
        * (np.arange(inner_size)[:, None] * np.arange(outer_size)[None, :] % length)
        / length
    )
    return (
        jnp.asarray(np.cos(angles), jnp.float32),
        jnp.asarray(direction * np.sin(angles), jnp.float32),
    )


def complex_step(real_part, imag_part, pattern, matrix):
    if imag_part is None:
        return (contract(pattern, real_part, matrix[0]), contract(pattern, real_part, matrix[1]))
    return (
        contract(pattern, real_part, matrix[0]) - contract(pattern, imag_part, matrix[1]),
        contract(pattern, real_part, matrix[1]) + contract(pattern, imag_part, matrix[0]),
    )


def data_gradient(sky_image, measured_real, measured_imaginary, sampling_mask):
    channels, row_count, column_count = sky_image.shape
    outer_size = 64
    inner_size = column_count // outer_size
    sample_grid = sky_image.reshape(channels, row_count, inner_size, outer_size)
    real_part, imag_part = complex_step(
        sample_grid, None, "crba,rs->csba", fourier_table(row_count, -1.0)
    )
    real_part, imag_part = complex_step(
        real_part, imag_part, "csba,bk->cska", fourier_table(inner_size, -1.0)
    )
    twist_real, twist_imag = twist_table(inner_size, outer_size, column_count, -1.0)
    real_part, imag_part = (
        real_part * twist_real - imag_part * twist_imag,
        real_part * twist_imag + imag_part * twist_real,
    )
    real_part, imag_part = complex_step(
        real_part, imag_part, "cska,aj->csjk", fourier_table(outer_size, -1.0)
    )
    weights = sampling_mask.astype(jnp.float32)
    real_part = weights * (real_part.reshape(channels, row_count, column_count) - measured_real)
    imag_part = weights * (
        imag_part.reshape(channels, row_count, column_count) - measured_imaginary
    )
    real_part = real_part.reshape(channels, row_count, outer_size, inner_size)
    imag_part = imag_part.reshape(channels, row_count, outer_size, inner_size)
    real_part, imag_part = complex_step(
        real_part, imag_part, "csjk,ja->cska", fourier_table(outer_size, 1.0)
    )
    twist_real, twist_imag = twist_table(inner_size, outer_size, column_count, 1.0)
    real_part, imag_part = (
        real_part * twist_real - imag_part * twist_imag,
        real_part * twist_imag + imag_part * twist_real,
    )
    real_part, imag_part = complex_step(
        real_part, imag_part, "cska,kb->csba", fourier_table(inner_size, 1.0)
    )
    row_real, row_imag = fourier_table(row_count, 1.0)
    result = contract("csba,sr->crba", real_part, row_real) - contract(
        "csba,sr->crba", imag_part, row_imag
    )
    return result.reshape(channels, row_count, column_count)


def row_matrix(length):
    current = np.eye(length)
    details = []
    for level_index in range(LEVELS):
        width_now = current.shape[0]
        half_size = width_now // 2
        lower = np.zeros((half_size, width_now))
        upper = np.zeros((half_size, width_now))
        for target in range(half_size):
            for tap_index in range(8):
                lower[target, (2 * target + tap_index) % width_now] += low_pass[tap_index]
                upper[target, (2 * target + tap_index) % width_now] += high_pass[tap_index]
        details.insert(0, upper @ current)
        current = lower @ current
    return jnp.asarray(np.concatenate([current] + details, 0), jnp.float32)


def analysis_step(length):
    half_size = length // 2
    matrix = np.zeros((length + 6, length))
    for target in range(half_size):
        for tap_index in range(8):
            matrix[2 * target + tap_index, target] += low_pass[tap_index]
            matrix[2 * target + tap_index, half_size + target] += high_pass[tap_index]
    return jnp.asarray(matrix, jnp.float32)


def synthesis_step(length):
    matrix = np.zeros((2 * (length + 3), 2 * length))
    for source in range(length):
        for parity in range(2):
            for back_step in range(4):
                matrix[source - back_step + 3, 2 * source + parity] += low_pass[
                    parity + 2 * back_step
                ]
                matrix[length + 3 + source - back_step + 3, 2 * source + parity] += high_pass[
                    parity + 2 * back_step
                ]
    return jnp.asarray(matrix, jnp.float32)


def column_analysis(values, right_rim):
    coarse = values
    details = []
    for level_index in range(LEVELS):
        length = coarse.shape[-1]
        extended = jnp.concatenate([coarse, right_rim(coarse[..., :6])], -1)
        halves = contract("...m,mk->...k", extended, analysis_step(length))
        details.insert(0, halves[..., length // 2 :])
        coarse = halves[..., : length // 2]
    return jnp.concatenate([coarse] + details, -1)


def column_synthesis(coefficients, left_rim):
    length = coefficients.shape[-1] >> LEVELS
    coarse = coefficients[..., :length]
    offset = length
    for level_index in range(LEVELS):
        detail = coefficients[..., offset : offset + length]
        coarse_edge, detail_edge = left_rim(coarse[..., -3:], detail[..., -3:])
        extended = jnp.concatenate([coarse_edge, coarse, detail_edge, detail], -1)
        coarse = contract("...m,mk->...k", extended, synthesis_step(length))
        offset = offset + length
        length = length * 2
    return coarse


def right_within(edge_cols):
    return jnp.roll(edge_cols, -1, axis=-2)


def left_within(coarse_edge, detail_edge):
    return (jnp.roll(coarse_edge, 1, axis=-2), jnp.roll(detail_edge, 1, axis=-2))


def shards(sky_image, measured_real, measured_imaginary, sampling_mask, dual_field):
    channels, row_count, column_count = sky_image.shape
    rows_table = row_matrix(row_count)
    gradient = data_gradient(sky_image, measured_real, measured_imaginary, sampling_mask)
    facet_count = lax.axis_size("fac")
    facet_width = column_count // facet_count
    local_dual = lax.all_to_all(dual_field, "fac", split_axis=0, concat_axis=2, tiled=True)
    coefficients = local_dual.reshape(channels, row_count, facet_count, facet_width)
    prior_term = column_synthesis(coefficients, left_within).reshape(
        channels, row_count, column_count
    )
    prior_term = contract("sr,csn->crn", rows_table, prior_term)
    next_image = jnp.maximum(sky_image - primal_step * (gradient + prior_term), 0.0)
    analysed = contract("rs,csn->crn", rows_table, 2.0 * next_image - sky_image)
    analysed = column_analysis(
        analysed.reshape(channels, row_count, facet_count, facet_width), right_within
    )
    lifted = local_dual + dual_step * analysed.reshape(channels, row_count, column_count)
    summed = lax.psum(jnp.sum(lifted * lifted, axis=0), "fac")
    shrunk = lifted / jnp.maximum(1.0, jnp.sqrt(summed) / ball_radius)
    next_dual = lax.all_to_all(shrunk, "fac", split_axis=2, concat_axis=0, tiled=True)
    return (next_image, next_dual)


def solution(mesh):
    return jax.shard_map(
        shards,
        mesh=mesh,
        in_specs=(
            P(("groups", "fac"), None, None),
            P(("groups", "fac"), None, None),
            P(("groups", "fac"), None, None),
            P(("groups", "fac"), None, None),
            P("groups", None, "fac"),
        ),
        out_specs=(P(("groups", "fac"), None, None), P("groups", None, "fac")),
        check_vma=False,
    )
```

profile of v0, /device:TPU:0, one launch (start us, length us, event | category | flops | bytes accessed | tf_op | source)
XLA Modules:
  0.0 563.5 jit_solution(9362236796377634353)
XLA Ops:
  7.2 7.4 %all-to-all-start = ((f32[64,96,128]{2,1,0:T(8,128)}), f32[64,96,128]{2,1,0:T(8,128)}, u32[]{:S(2)}, u32[]{:S(2)}) async-start(f32[64,96,128]{2,1,0:T(8,128)} %param.34), calls=%async_computation | async-start | bytes 6291456 | tf_op jit(solution)/shard_map/all_to_all | solution.py:188
  34.0 6.8 %fusion.35 = f32[2,96,64,64]{1,3,2,0:T(8,128)S(1)} fusion(f32[64,64,1,1]{0,1,3,2:T(8,128)S(1)} %copy-done.10, f32[2,96,64,64]{1,3,2,0:T(8,128)S(1)} %bitcast.155), kind=kOutput, calls=%fused_computation.54 | convolution fusion | flops 603979776 | bytes 6307840 | tf_op jit(solution)/shard_map/csba,bk->cska/dot_general | solution.py:26
  40.8 6.6 %fusion.60 = f32[2,96,64,64]{1,3,2,0:T(8,128)S(1)} fusion(f32[2,96,64,64]{1,3,2,0:T(8,128)S(1)} %fusion.37, f32[64,64,1,1]{0,1,3,2:T(8,128)S(1)} %copy-done.10, f32[2,96,64,64]{1,3,2,0:T(8,128)S(1)} %bitcast.152), kind=kOutput, calls=%fused_computation.80 | convolution fusion | flops 604766208 | bytes 9453568 | tf_op jit(solution)/shard_map/csba,bk->cska/dot_general | solution.py:26
  47.5 11.3 %fusion.13 = (f32[2,96,64,64]{1,2,3,0:T(8,128)}, f32[2,96,64,64]{1,2,3,0:T(8,128)S(1)}) fusion(f32[2,96,64,64]{1,3,2,0:T(8,128)S(1)} %fusion.60, f32[64,64]{0,1:T(8,128)S(1)} %copy-done.15, f32[64,64]{0,1:T(8,128)S(1)} %copy-done.9, f32[2,96,64,64]{1,3,2,0:T(8,128)S(1)} %fusion.35, f32[64,64,1,1]{0,1,3,2:T(8,128)S(1)} %copy-done.13, ...), kind=kOutput, calls=%fused_computation.20 | convolution fusion | flops 609484800 | bytes 15777792 | tf_op jit(solution)/shard_map/csba,bk->cska/dot_general | solution.py:26
  58.7 7.1 %fusion.29 = f32[2,96,64,64]{1,3,2,0:T(8,128)} fusion(f32[64,64,1,1]{0,1,3,2:T(8,128)S(1)} %copy-done.13, f32[2,96,64,64]{1,2,3,0:T(8,128)S(1)} %get-tuple-element.5), kind=kOutput, calls=%fused_computation.48 | convolution fusion | flops 603979776 | bytes 6307840 | tf_op jit(solution)/shard_map/cska,aj->csjk/dot_general | solution.py:26
  65.8 7.1 %fusion.27 = f32[2,96,64,64]{1,3,2,0:T(8,128)} fusion(f32[64,64,1,1]{0,1,3,2:T(8,128)S(1)} %copy-done.10, f32[2,96,64,64]{1,2,3,0:T(8,128)S(1)} %get-tuple-element.5), kind=kOutput, calls=%fused_computation.46 | convolution fusion | flops 603979776 | bytes 6307840 | tf_op jit(solution)/shard_map/cska,aj->csjk/dot_general | solution.py:26
  78.2 9.7 %subtract_bitcast_fusion.1 = f32[2,96,64,64]{1,2,3,0:T(8,128)S(1)} fusion(f32[2,96,64,64]{1,3,2,0:T(8,128)} %fusion.29, f32[64,64,1,1]{0,1,3,2:T(8,128)S(1)} %copy-done.10, f32[2,96,64,64]{1,2,3,0:T(8,128)} %get-tuple-element.4), kind=kOutput, calls=%fused_computation.37 | convolution fusion | flops 604766208 | bytes 9453568 | tf_op jit(solution)/shard_map/cska,aj->csjk/dot_general | solution.py:26
  102.7 9.7 %add_bitcast_fusion.1 = f32[2,96,64,64]{1,2,3,0:T(8,128)S(1)} fusion(f32[2,96,64,64]{1,3,2,0:T(8,128)} %fusion.27, f32[64,64,1,1]{0,1,3,2:T(8,128)S(1)} %copy-done.13, f32[2,96,64,64]{1,2,3,0:T(8,128)} %get-tuple-element.4), kind=kOutput, calls=%fused_computation.36 | convolution fusion | flops 604766208 | bytes 9453568 | tf_op jit(solution)/shard_map/cska,aj->csjk/dot_general | solution.py:26
  116.7 11.3 %fusion.12 = (f32[2,96,4096]{1,2,0:T(8,128)}, f32[2,96,4096]{1,2,0:T(8,128)}) fusion(f32[2,96,4096]{1,2,0:T(8,128)} %copy.132, f32[2,96,64,64]{1,3,2,0:T(8,128)} %copy.131, s32[2,96,4096]{1,2,0:T(8,128)} %copy.123, f32[2,96,4096]{1,2,0:T(8,128)} %copy.137, f32[2,96,64,64]{1,3,2,0:T(8,128)} %copy.136), kind=kLoop, calls=%fused_computation.17 | loop fusion | flops 3932160 | bytes 22020096 | tf_op jit(solution)/shard_map/mul | solution.py:83
  128.0 10.9 %fusion.19 = f32[2,96,64,64]{1,3,2,0:T(8,128)} fusion(f32[64,64,1,1]{0,1,3,2:T(8,128)S(1)} %copy-done.10, f32[2,96,64,64]{1,3,2,0:T(8,128)} %bitcast.164), kind=kOutput, calls=%fused_computation.38 | convolution fusion | flops 603979776 | bytes 6307840 | tf_op jit(solution)/shard_map/csjk,ja->cska/dot_general | solution.py:26
  138.9 7.1 %fusion.21 = f32[2,96,64,64]{1,3,2,0:T(8,128)} fusion(f32[64,64,1,1]{0,1,3,2:T(8,128)S(1)} %copy-done.12, f32[2,96,64,64]{1,3,2,0:T(8,128)S(1)} %bitcast.165), kind=kOutput, calls=%fused_computation.40 | convolution fusion | flops 603979776 | bytes 6307840 | tf_op jit(solution)/shard_map/csjk,ja->cska/dot_general | solution.py:26
  146.0 7.1 %fusion.23 = f32[2,96,64,64]{1,3,2,0:T(8,128)} fusion(f32[64,64,1,1]{0,1,3,2:T(8,128)S(1)} %copy-done.12, f32[2,96,64,64]{1,3,2,0:T(8,128)S(1)} %bitcast.162), kind=kOutput, calls=%fused_computation.42 | convolution fusion | flops 603979776 | bytes 6307840 | tf_op jit(solution)/shard_map/csjk,ja->cska/dot_general | solution.py:26
  153.1 7.2 %fusion.25 = f32[2,96,64,64]{1,3,2,0:T(8,128)} fusion(f32[64,64,1,1]{0,1,3,2:T(8,128)S(1)} %copy-done.10, f32[2,96,64,64]{1,3,2,0:T(8,128)S(1)} %bitcast.163), kind=kOutput, calls=%fused_computation.44 | convolution fusion | flops 603979776 | bytes 6307840 | tf_op jit(solution)/shard_map/csjk,ja->cska/dot_general | solution.py:26
  160.3 17.0 %copy_add_fusion = (f32[2,96,64,64]{1,2,3,0:T(8,128)S(1)}, f32[2,96,64,64]{1,2,3,0:T(8,128)}) fusion(f32[2,96,64,64]{1,3,2,0:T(8,128)} %fusion.19, f32[2,96,64,64]{1,3,2,0:T(8,128)} %fusion.23, f32[2,96,64,64]{1,3,2,0:T(8,128)} %fusion.21, f32[2,96,64,64]{1,3,2,0:T(8,128)} %fusion.25), kind=kLoop, calls=%fused_computation.29 | loop fusion | flops 1572864 | bytes 18874368 | tf_op jit(solution)/shard_map/add | solution.py:59
  177.3 6.7 %fusion.74 = f32[2,96,64,64]{1,3,2,0:T(8,128)S(1)} fusion(f32[64,64,1,1]{0,1,3,2:T(8,128)S(1)} %copy-done.12, f32[2,96,64,64]{1,2,3,0:T(8,128)S(1)} %get-tuple-element.26, f32[2,96,64,64]{1,2,3,0:T(8,128)} %get-tuple-element.27, f32[64,64]{0,1:T(8,128)S(1)} %copy-done.11, f32[64,64]{0,1:T(8,128)S(1)} %copy-done.9), kind=kOutput, calls=%fused_computation.85 | convolution fusion | flops 606339072 | bytes 9486336 | tf_op jit(solution)/shard_map/cska,kb->csba/dot_general | solution.py:26
  206.8 7.4 %fusion.70 = f32[2,64,64,96]{3,2,1,0:T(8,128)} fusion(f32[2,64,64,96]{3,2,1,0:T(8,128)S(1)} %fusion.15, f32[96,96,1,1]{1,0,3,2:T(8,128)S(1)} %copy-done.18, f32[2,96,64,64]{1,2,3,0:T(8,128)S(1)} %subtract_bitcast_fusion), kind=kOutput, calls=%fused_computation.82 | convolution fusion | flops 906756096 | bytes 9474048 | tf_op jit(solution)/shard_map/csba,sr->crba/dot_general | solution.py:26
  235.5 7.8 %copy.148 = f32[2,96,32,134]{3,2,1,0:T(8,128)} copy(f32[2,96,32,134]{1,3,2,0:T(8,128)} %pad_maximum_fusion) | data formatting | bytes 6586368 | tf_op jit(solution)/shard_map/concatenate | solution.py:167
  243.3 8.3 %fusion.128 = f32[2,96,32,128]{3,2,1,0:T(8,128)} fusion(f32[2,96,32,134]{3,2,1,0:T(8,128)} %copy.148, f32[134,128,1,1]{1,0,3,2:T(8,128)S(1)} %copy-done.17), kind=kOutput, calls=%fused_computation.138 | convolution fusion | flops 1264582656 | bytes 6507520 | tf_op jit(solution)/shard_map/...m,mk->...k/dot_general | solution.py:26
  276.0 8.4 %fusion.43 = f32[2,96,32,64]{1,3,2,0:T(8,128)S(1)} fusion(f32[70,64,1,1]{0,1,3,2:T(8,128)S(1)} %copy-done.22, f32[2,96,32,70]{3,2,1,0:T(8,128)S(1)} %maximum_maximum_fusion), kind=kOutput, calls=%fused_computation.63 | convolution fusion | flops 330301440 | bytes 3311104 | tf_op jit(solution)/shard_map/...m,mk->...k/dot_general | solution.py:26
  292.7 7.0 %multiply_reduce_fusion = (f32[96,32,128]{0,2,1:T(8,128)}, f32[2,96,32,128]{1,3,2,0:T(8,128)}) fusion(f32[2,96,32,64]{1,3,2,0:T(8,128)} %copy.170, f32[2,96,32,32]{1,3,2,0:T(8,128)} %get-tuple-element.23, f32[2,96,32,16]{1,3,2,0:T(8,128)} %get-tuple-element.25, f32[2,96,32,16]{1,3,2,0:T(8,128)S(1)} %fusion.106, f32[32,2,96,128]{2,3,0,1:T(8,128)} %copy.147), kind=kLoop, calls=%fused_computation.31 | loop fusion | flops 5111808 | bytes 11010048 | tf_op jit(solution)/shard_map/reduce_sum | solution.py:200
  299.6 135.1 %all-reduce.2.cloned.1.call-done = f32[96,4096]{0,1:T(8,128)} async-done(((f32[96,4096]{0,1:T(8,128)}), f32[96,4096]{0,1:T(8,128)}) %all-reduce.2.cloned.1.call-update) | async-done | bytes 1572880 | tf_op jit(solution)/shard_map/psum | solution.py:200
  437.6 15.1 %copy_divide_fusion = f32[2,96,4096]{1,0,2:T(2,128)S(1)} fusion(f32[2,96,4096]{1,2,0:T(8,128)S(1)} %bitcast.169, f32[96,4096]{0,1:T(8,128)S(1)} %multiply_maximum_fusion), kind=kLoop, calls=%fused_computation.24 | loop fusion | flops 786432 | bytes 7864320 | tf_op jit(solution)/shard_map/div | solution.py:201
  452.7 97.1 %all_to_all.33 = f32[2,96,4096]{1,0,2:T(2,128)} all-to-all(f32[2,96,4096]{1,0,2:T(2,128)S(1)} %copy_divide_fusion), channel_id=1, replica_groups=mesh['groups'=1,'fac'=32] {'fac'}, dimensions={2} | all-to-all | bytes 6291456 | tf_op jit(solution)/shard_map/all_to_all | solution.py:202
  549.8 6.6 %copy.154 = f32[32,2,96,128]{3,2,1,0:T(8,128)} copy(f32[32,2,96,128]{2,1,3,0:T(2,128)} %bitcast.171) | data formatting | bytes 6291456 | tf_op jit(solution)/shard_map/all_to_all | solution.py:202
  (111 shorter events, 123.0 us)
Async XLA Ops:
  7.2 7.5 %copy-start.5 = (f32[2,96,4096]{2,1,0:T(8,128)S(1)}, f32[2,96,4096]{2,1,0:T(8,128)}, u32[]{:S(2)}) copy-start(f32[2,96,4096]{2,1,0:T(8,128)} %param.30) | copy-start | bytes 9437188
  7.2 212.3 %all-to-all-start = ((f32[64,96,128]{2,1,0:T(8,128)}), f32[64,96,128]{2,1,0:T(8,128)}, u32[]{:S(2)}, u32[]{:S(2)}) async-start(f32[64,96,128]{2,1,0:T(8,128)} %param.34), calls=%async_computation | async-start | bytes 6291456 | tf_op jit(solution)/shard_map/all_to_all | solution.py:188
  14.6 3.4 copy-start.20
  14.6 420.1 %all-reduce.2.cloned.1.call-start = ((), (), s32[]{:S(2)}) async-start(), calls=%async_computation.2 | async-start | bytes 4194304 | tf_op jit(solution)/shard_map/psum | solution.py:200
  18.0 5.8 %copy-start.1 = (f32[2,96,4096]{1,2,0:T(8,128)S(1)}, f32[2,96,4096]{1,2,0:T(8,128)}, u32[]{:S(2)}) copy-start(f32[2,96,4096]{1,2,0:T(8,128)} %copy.124) | copy-start | bytes 9437188
  18.0 5.8 %copy-start.21 = (f32[96,96]{1,0:T(8,128)S(1)}, f32[96,96]{1,0:T(8,128)}, u32[]{:S(2)}) copy-start(f32[96,96]{1,0:T(8,128)} %constant.51.clone) | copy-start | bytes 110596
  23.8 3.6 copy-start.13
  27.4 6.6 %copy-start.10 = (f32[64,64,1,1]{0,1,3,2:T(8,128)S(1)}, f32[64,64,1,1]{0,1,3,2:T(8,128)}, u32[]{:S(2)}) copy-start(f32[64,64,1,1]{0,1,3,2:T(8,128)} %constant.72) | copy-start | bytes 49156
  40.8 6.6 %copy-start.9 = (f32[64,64]{0,1:T(8,128)S(1)}, f32[64,64]{0,1:T(8,128)}, u32[]{:S(2)}) copy-start(f32[64,64]{0,1:T(8,128)} %constant.55.clone) | copy-start | bytes 49156
  40.8 6.6 %copy-start.15 = (f32[64,64]{0,1:T(8,128)S(1)}, f32[64,64]{0,1:T(8,128)}, u32[]{:S(2)}) copy-start(f32[64,64]{0,1:T(8,128)} %constant.56.clone) | copy-start | bytes 49156
  128.0 10.9 %copy-start.4 = (f32[2,96,4096]{1,2,0:T(8,128)S(1)}, f32[2,96,4096]{1,2,0:T(8,128)}, u32[]{:S(2)}) copy-start(f32[2,96,4096]{1,2,0:T(8,128)} %get-tuple-element.19) | copy-start | bytes 9437188
  128.0 10.9 %copy-start.12 = (f32[64,64,1,1]{0,1,3,2:T(8,128)S(1)}, f32[64,64,1,1]{0,1,3,2:T(8,128)}, u32[]{:S(2)}) copy-start(f32[64,64,1,1]{0,1,3,2:T(8,128)} %constant.74) | copy-start | bytes 49156
  138.9 7.1 %copy-start.3 = (f32[2,96,4096]{1,2,0:T(8,128)S(1)}, f32[2,96,4096]{1,2,0:T(8,128)}, u32[]{:S(2)}) copy-start(f32[2,96,4096]{1,2,0:T(8,128)} %get-tuple-element.18) | copy-start | bytes 9437188
  160.3 17.0 %copy-start.11 = (f32[64,64]{0,1:T(8,128)S(1)}, f32[64,64]{0,1:T(8,128)}, u32[]{:S(2)}) copy-start(f32[64,64]{0,1:T(8,128)} %constant.58.clone) | copy-start | bytes 49156
  177.3 6.7 %copy-start = (f32[2,96,64,64]{1,2,3,0:T(8,128)S(1)}, f32[2,96,64,64]{1,2,3,0:T(8,128)}, u32[]{:S(2)}) copy-start(f32[2,96,64,64]{1,2,3,0:T(8,128)} %get-tuple-element.27) | copy-start | bytes 9437188
  184.0 5.6 copy-start.19
  201.5 5.4 copy-start.18
  224.7 3.2 copy-start.27
  235.5 7.8 %copy-start.17 = (f32[134,128,1,1]{1,0,3,2:T(8,128)S(1)}, f32[134,128,1,1]{1,0,3,2:T(8,128)}, u32[]{:S(2)}) copy-start(f32[134,128,1,1]{1,0,3,2:T(8,128)} %constant.80) | copy-start | bytes 205828
  251.6 4.9 copy-start.6
  251.6 5.0 copy-start.14
  262.8 3.4 copy-start.8
  276.0 9.6 %copy-start.23 = (f32[38,32,1,1]{0,1,3,2:T(8,128)S(1)}, f32[38,32,1,1]{0,1,3,2:T(8,128)}, u32[]{:S(2)}) copy-start(f32[38,32,1,1]{0,1,3,2:T(8,128)} %constant.84) | copy-start | bytes 14596
  286.7 4.2 copy-start.24
  (6 other events, 11.5 us)
Sparse Core Ops, SparseCore 0:
  299.8 134.9 all-reduce.1
where the time goes:
time: 567 us; the launch traced here: 563 us
  matrix products  183 us (32%)
  waiting for transfers between devices  135 us (24%)
  blocking collectives  97.1 us (17%)
  local copies, waits for them, and re-layouts  69.9 us (12%)
  other arithmetic  56.4 us (10%)
  between operations  14.9 us (3%)
  starting transfers between devices  7.46 us (1%)
    dot_general x28, matrix products, contract(): jnp.einsum(pattern, left_side, right_side, precision=precise, preferred_e...  173 us
    psum x1, waiting for transfers between devices, shards(): summed = lax.psum(jnp.sum(lifted * lifted, axis=0), 'fac')  135 us
    all_to_all x1, blocking collectives, shards(): lax.all_to_all(shrunk, 'fac', split_axis=2, concat_axis=0, tiled=True)  97.1 us
    unnamed x62, local copies, waits for them, and re-layouts  24.6 us
    add x1, other arithmetic, complex_step(): contract(pattern, real_part, matrix[1])  17 us
    div x1, other arithmetic, shards(): shrunk = lifted / jnp.maximum(1.0, jnp.sqrt(summed) / ball_radius)  15.1 us
  transfers between devices with their start and end apart: 2, of which 1 were waited for; matrix products, arithmetic and copies ran while one was open for 36% of the time, Pallas kernels for 0%

commit v1 on v0

--- a/solution.py
+++ b/solution.py
@@ -185,7 +185,10 @@
     gradient = data_gradient(sky_image, measured_real, measured_imaginary, sampling_mask)
     facet_count = lax.axis_size("fac")
     facet_width = column_count // facet_count
-    local_dual = lax.all_to_all(dual_field, "fac", split_axis=0, concat_axis=2, tiled=True)
+    local_dual = jnp.concatenate(
+        lax.all_to_all(jnp.stack(jnp.split(dual_field, lax.axis_size("fac"), axis=0)), "fac", 0, 0),
+        axis=2,
+    )
     coefficients = local_dual.reshape(channels, row_count, facet_count, facet_width)
     prior_term = column_synthesis(coefficients, left_within).reshape(
         channels, row_count, column_count

time: 567 us -> 618 us (1.090)
  local copies, waits for them, and re-layouts: 69.9 us -> 119 us
    unnamed x62 -> x93, local copies, waits for them, and re-layouts: 24.6 us -> 72.4 us
  transfers between devices with their start and end apart: 2 -> 2, of which waited for: 1 -> 1; matrix products, arithmetic and copies ran while one was open for 36% -> 33% of each run, Pallas kernels for 0% -> 0%
where the time goes in v1:
time: 618 us; the launch traced here: 613 us
  matrix products  183 us (30%)
  waiting for transfers between devices  135 us (22%)
  local copies, waits for them, and re-layouts  119 us (19%)
  blocking collectives  97.1 us (16%)
  other arithmetic  56.4 us (9%)
  between operations  14.9 us (2%)
  starting transfers between devices  7.45 us (1%)
    dot_general x28, matrix products, contract(): jnp.einsum(pattern, left_side, right_side, precision=precise, preferred_e...  173 us
    psum x1, waiting for transfers between devices, shards(): summed = lax.psum(jnp.sum(lifted * lifted, axis=0), 'fac')  135 us
    all_to_all x1, blocking collectives, shards(): lax.all_to_all(shrunk, 'fac', split_axis=2, concat_axis=0, tiled=True)  97.1 us
    unnamed x93, local copies, waits for them, and re-layouts  72.4 us
    add x1, other arithmetic, complex_step(): contract(pattern, real_part, matrix[1])  17 us
    div x1, other arithmetic, shards(): shrunk = lifted / jnp.maximum(1.0, jnp.sqrt(summed) / ball_radius)  15.1 us
  transfers between devices with their start and end apart: 2, of which 1 were waited for; matrix products, arithmetic and copies ran while one was open for 33% of the time, Pallas kernels for 0%

profile of v1, /device:TPU:0, one launch (start us, length us, event | category | flops | bytes accessed | tf_op | source)
XLA Modules:
  0.0 612.9 jit_solution(10371218485542925350)
XLA Ops:
  56.6 7.4 %all-to-all-start = ((f32[32,2,96,128]{3,2,1,0:T(8,128)}), f32[32,2,96,128]{3,2,1,0:T(8,128)}, u32[]{:S(2)}, u32[]{:S(2)}) async-start(f32[32,2,96,128]{3,2,1,0:T(8,128)} %bitcast_dynamic-update-slice_fusion), calls=%async_computation | async-start | bytes 6291456 | tf_op jit(solution)/shard_map/all_to_all | solution.py:189
  83.4 6.8 %fusion.35 = f32[2,96,64,64]{1,3,2,0:T(8,128)S(1)} fusion(f32[64,64,1,1]{0,1,3,2:T(8,128)S(1)} %copy-done.10, f32[2,96,64,64]{1,3,2,0:T(8,128)S(1)} %bitcast.218), kind=kOutput, calls=%fused_computation.54 | convolution fusion | flops 603979776 | bytes 6307840 | tf_op jit(solution)/shard_map/csba,bk->cska/dot_general | solution.py:26
  90.2 6.6 %fusion.60 = f32[2,96,64,64]{1,3,2,0:T(8,128)S(1)} fusion(f32[2,96,64,64]{1,3,2,0:T(8,128)S(1)} %fusion.37, f32[64,64,1,1]{0,1,3,2:T(8,128)S(1)} %copy-done.10, f32[2,96,64,64]{1,3,2,0:T(8,128)S(1)} %bitcast.215), kind=kOutput, calls=%fused_computation.80 | convolution fusion | flops 604766208 | bytes 9453568 | tf_op jit(solution)/shard_map/csba,bk->cska/dot_general | solution.py:26
  96.9 11.2 %fusion.13 = (f32[2,96,64,64]{1,2,3,0:T(8,128)}, f32[2,96,64,64]{1,2,3,0:T(8,128)S(1)}) fusion(f32[2,96,64,64]{1,3,2,0:T(8,128)S(1)} %fusion.60, f32[64,64]{0,1:T(8,128)S(1)} %copy-done.15, f32[64,64]{0,1:T(8,128)S(1)} %copy-done.9, f32[2,96,64,64]{1,3,2,0:T(8,128)S(1)} %fusion.35, f32[64,64,1,1]{0,1,3,2:T(8,128)S(1)} %copy-done.13, ...), kind=kOutput, calls=%fused_computation.20 | convolution fusion | flops 609484800 | bytes 15777792 | tf_op jit(solution)/shard_map/csba,bk->cska/dot_general | solution.py:26
  108.1 7.0 %fusion.29 = f32[2,96,64,64]{1,3,2,0:T(8,128)} fusion(f32[64,64,1,1]{0,1,3,2:T(8,128)S(1)} %copy-done.13, f32[2,96,64,64]{1,2,3,0:T(8,128)S(1)} %get-tuple-element.5), kind=kOutput, calls=%fused_computation.48 | convolution fusion | flops 603979776 | bytes 6307840 | tf_op jit(solution)/shard_map/cska,aj->csjk/dot_general | solution.py:26
  115.1 7.1 %fusion.27 = f32[2,96,64,64]{1,3,2,0:T(8,128)} fusion(f32[64,64,1,1]{0,1,3,2:T(8,128)S(1)} %copy-done.10, f32[2,96,64,64]{1,2,3,0:T(8,128)S(1)} %get-tuple-element.5), kind=kOutput, calls=%fused_computation.46 | convolution fusion | flops 603979776 | bytes 6307840 | tf_op jit(solution)/shard_map/cska,aj->csjk/dot_general | solution.py:26
  127.5 9.7 %subtract_bitcast_fusion.1 = f32[2,96,64,64]{1,2,3,0:T(8,128)S(1)} fusion(f32[2,96,64,64]{1,3,2,0:T(8,128)} %fusion.29, f32[64,64,1,1]{0,1,3,2:T(8,128)S(1)} %copy-done.10, f32[2,96,64,64]{1,2,3,0:T(8,128)} %get-tuple-element.4), kind=kOutput, calls=%fused_computation.37 | convolution fusion | flops 604766208 | bytes 9453568 | tf_op jit(solution)/shard_map/cska,aj->csjk/dot_general | solution.py:26
  152.1 9.7 %add_bitcast_fusion.1 = f32[2,96,64,64]{1,2,3,0:T(8,128)S(1)} fusion(f32[2,96,64,64]{1,3,2,0:T(8,128)} %fusion.27, f32[64,64,1,1]{0,1,3,2:T(8,128)S(1)} %copy-done.13, f32[2,96,64,64]{1,2,3,0:T(8,128)} %get-tuple-element.4), kind=kOutput, calls=%fused_computation.36 | convolution fusion | flops 604766208 | bytes 9453568 | tf_op jit(solution)/shard_map/cska,aj->csjk/dot_general | solution.py:26
  166.1 11.3 %fusion.12 = (f32[2,96,4096]{1,2,0:T(8,128)}, f32[2,96,4096]{1,2,0:T(8,128)}) fusion(f32[2,96,4096]{1,2,0:T(8,128)} %copy.195, f32[2,96,64,64]{1,3,2,0:T(8,128)} %copy.194, s32[2,96,4096]{1,2,0:T(8,128)} %copy.186, f32[2,96,4096]{1,2,0:T(8,128)} %copy.200, f32[2,96,64,64]{1,3,2,0:T(8,128)} %copy.199), kind=kLoop, calls=%fused_computation.17 | loop fusion | flops 3932160 | bytes 22020096 | tf_op jit(solution)/shard_map/mul | solution.py:83
  177.4 10.9 %fusion.19 = f32[2,96,64,64]{1,3,2,0:T(8,128)} fusion(f32[64,64,1,1]{0,1,3,2:T(8,128)S(1)} %copy-done.10, f32[2,96,64,64]{1,3,2,0:T(8,128)} %bitcast.227), kind=kOutput, calls=%fused_computation.38 | convolution fusion | flops 603979776 | bytes 6307840 | tf_op jit(solution)/shard_map/csjk,ja->cska/dot_general | solution.py:26
  188.3 7.1 %fusion.21 = f32[2,96,64,64]{1,3,2,0:T(8,128)} fusion(f32[64,64,1,1]{0,1,3,2:T(8,128)S(1)} %copy-done.12, f32[2,96,64,64]{1,3,2,0:T(8,128)S(1)} %bitcast.228), kind=kOutput, calls=%fused_computation.40 | convolution fusion | flops 603979776 | bytes 6307840 | tf_op jit(solution)/shard_map/csjk,ja->cska/dot_general | solution.py:26
  195.3 7.1 %fusion.23 = f32[2,96,64,64]{1,3,2,0:T(8,128)} fusion(f32[64,64,1,1]{0,1,3,2:T(8,128)S(1)} %copy-done.12, f32[2,96,64,64]{1,3,2,0:T(8,128)S(1)} %bitcast.225), kind=kOutput, calls=%fused_computation.42 | convolution fusion | flops 603979776 | bytes 6307840 | tf_op jit(solution)/shard_map/csjk,ja->cska/dot_general | solution.py:26
  202.5 7.2 %fusion.25 = f32[2,96,64,64]{1,3,2,0:T(8,128)} fusion(f32[64,64,1,1]{0,1,3,2:T(8,128)S(1)} %copy-done.10, f32[2,96,64,64]{1,3,2,0:T(8,128)S(1)} %bitcast.226), kind=kOutput, calls=%fused_computation.44 | convolution fusion | flops 603979776 | bytes 6307840 | tf_op jit(solution)/shard_map/csjk,ja->cska/dot_general | solution.py:26
  209.7 17.0 %copy_add_fusion = (f32[2,96,64,64]{1,2,3,0:T(8,128)S(1)}, f32[2,96,64,64]{1,2,3,0:T(8,128)}) fusion(f32[2,96,64,64]{1,3,2,0:T(8,128)} %fusion.19, f32[2,96,64,64]{1,3,2,0:T(8,128)} %fusion.23, f32[2,96,64,64]{1,3,2,0:T(8,128)} %fusion.21, f32[2,96,64,64]{1,3,2,0:T(8,128)} %fusion.25), kind=kLoop, calls=%fused_computation.29 | loop fusion | flops 1572864 | bytes 18874368 | tf_op jit(solution)/shard_map/add | solution.py:59
  226.7 6.7 %fusion.74 = f32[2,96,64,64]{1,3,2,0:T(8,128)S(1)} fusion(f32[64,64,1,1]{0,1,3,2:T(8,128)S(1)} %copy-done.12, f32[2,96,64,64]{1,2,3,0:T(8,128)S(1)} %get-tuple-element.26, f32[2,96,64,64]{1,2,3,0:T(8,128)} %get-tuple-element.27, f32[64,64]{0,1:T(8,128)S(1)} %copy-done.11, f32[64,64]{0,1:T(8,128)S(1)} %copy-done.9), kind=kOutput, calls=%fused_computation.85 | convolution fusion | flops 606339072 | bytes 9486336 | tf_op jit(solution)/shard_map/cska,kb->csba/dot_general | solution.py:26
  256.2 7.4 %fusion.70 = f32[2,64,64,96]{3,2,1,0:T(8,128)} fusion(f32[2,64,64,96]{3,2,1,0:T(8,128)S(1)} %fusion.15, f32[96,96,1,1]{1,0,3,2:T(8,128)S(1)} %copy-done.18, f32[2,96,64,64]{1,2,3,0:T(8,128)S(1)} %subtract_bitcast_fusion), kind=kOutput, calls=%fused_computation.82 | convolution fusion | flops 906756096 | bytes 9474048 | tf_op jit(solution)/shard_map/csba,sr->crba/dot_general | solution.py:26
  284.9 7.8 %copy.211 = f32[2,96,32,134]{3,2,1,0:T(8,128)} copy(f32[2,96,32,134]{1,3,2,0:T(8,128)} %pad_maximum_fusion) | data formatting | bytes 6586368 | tf_op jit(solution)/shard_map/concatenate | solution.py:167
  292.7 8.3 %fusion.128 = f32[2,96,32,128]{3,2,1,0:T(8,128)} fusion(f32[2,96,32,134]{3,2,1,0:T(8,128)} %copy.211, f32[134,128,1,1]{1,0,3,2:T(8,128)S(1)} %copy-done.17), kind=kOutput, calls=%fused_computation.170 | convolution fusion | flops 1264582656 | bytes 6507520 | tf_op jit(solution)/shard_map/...m,mk->...k/dot_general | solution.py:26
  325.3 8.4 %fusion.43 = f32[2,96,32,64]{1,3,2,0:T(8,128)S(1)} fusion(f32[70,64,1,1]{0,1,3,2:T(8,128)S(1)} %copy-done.22, f32[2,96,32,70]{3,2,1,0:T(8,128)S(1)} %maximum_maximum_fusion), kind=kOutput, calls=%fused_computation.63 | convolution fusion | flops 330301440 | bytes 3311104 | tf_op jit(solution)/shard_map/...m,mk->...k/dot_general | solution.py:26
  342.0 7.0 %multiply_reduce_fusion = (f32[96,32,128]{0,2,1:T(8,128)}, f32[2,96,32,128]{1,3,2,0:T(8,128)}) fusion(f32[2,96,32,64]{1,3,2,0:T(8,128)} %copy.233, f32[2,96,32,32]{1,3,2,0:T(8,128)} %get-tuple-element.23, f32[2,96,32,16]{1,3,2,0:T(8,128)} %get-tuple-element.25, f32[2,96,32,16]{1,3,2,0:T(8,128)S(1)} %fusion.106, f32[32,2,96,128]{2,3,0,1:T(8,128)} %copy.210), kind=kLoop, calls=%fused_computation.31 | loop fusion | flops 5111808 | bytes 11010048 | tf_op jit(solution)/shard_map/reduce_sum | solution.py:203
  349.0 135.1 %all-reduce.2.cloned.1.call-done = f32[96,4096]{0,1:T(8,128)} async-done(((f32[96,4096]{0,1:T(8,128)}), f32[96,4096]{0,1:T(8,128)}) %all-reduce.2.cloned.1.call-update) | async-done | bytes 1572880 | tf_op jit(solution)/shard_map/psum | solution.py:203
  487.0 15.1 %copy_divide_fusion = f32[2,96,4096]{1,0,2:T(2,128)S(1)} fusion(f32[2,96,4096]{1,2,0:T(8,128)S(1)} %bitcast.232, f32[96,4096]{0,1:T(8,128)S(1)} %multiply_maximum_fusion), kind=kLoop, calls=%fused_computation.24 | loop fusion | flops 786432 | bytes 7864320 | tf_op jit(solution)/shard_map/div | solution.py:204
  502.1 97.1 %all_to_all.23 = f32[2,96,4096]{1,0,2:T(2,128)} all-to-all(f32[2,96,4096]{1,0,2:T(2,128)S(1)} %copy_divide_fusion), channel_id=1, replica_groups=mesh['groups'=1,'fac'=32] {'fac'}, dimensions={2} | all-to-all | bytes 6291456 | tf_op jit(solution)/shard_map/all_to_all | solution.py:205
  599.2 6.6 %copy.217 = f32[32,2,96,128]{3,2,1,0:T(8,128)} copy(f32[32,2,96,128]{2,1,3,0:T(2,128)} %bitcast.234) | data formatting | bytes 6291456 | tf_op jit(solution)/shard_map/all_to_all | solution.py:205
  (143 shorter events, 172.4 us)
Async XLA Ops:
  39.5 24.6 %copy-start.5 = (f32[2,96,4096]{2,1,0:T(8,128)S(1)}, f32[2,96,4096]{2,1,0:T(8,128)}, u32[]{:S(2)}) copy-start(f32[2,96,4096]{2,1,0:T(8,128)} %param.30) | copy-start | bytes 9437188
  56.6 212.3 %all-to-all-start = ((f32[32,2,96,128]{3,2,1,0:T(8,128)}), f32[32,2,96,128]{3,2,1,0:T(8,128)}, u32[]{:S(2)}, u32[]{:S(2)}) async-start(f32[32,2,96,128]{3,2,1,0:T(8,128)} %bitcast_dynamic-update-slice_fusion), calls=%async_computation | async-start | bytes 6291456 | tf_op jit(solution)/shard_map/all_to_all | solution.py:189
  64.0 3.4 copy-start.20
  64.0 420.2 %all-reduce.2.cloned.1.call-start = ((), (), s32[]{:S(2)}) async-start(), calls=%async_computation.2 | async-start | bytes 4194304 | tf_op jit(solution)/shard_map/psum | solution.py:203
  67.4 5.8 copy-start.1
  67.4 5.8 copy-start.21
  73.2 3.6 copy-start.13
  76.8 6.6 %copy-start.10 = (f32[64,64,1,1]{0,1,3,2:T(8,128)S(1)}, f32[64,64,1,1]{0,1,3,2:T(8,128)}, u32[]{:S(2)}) copy-start(f32[64,64,1,1]{0,1,3,2:T(8,128)} %constant.72) | copy-start | bytes 49156
  90.2 6.6 %copy-start.9 = (f32[64,64]{0,1:T(8,128)S(1)}, f32[64,64]{0,1:T(8,128)}, u32[]{:S(2)}) copy-start(f32[64,64]{0,1:T(8,128)} %constant.55.clone) | copy-start | bytes 49156
  90.2 6.6 %copy-start.15 = (f32[64,64]{0,1:T(8,128)S(1)}, f32[64,64]{0,1:T(8,128)}, u32[]{:S(2)}) copy-start(f32[64,64]{0,1:T(8,128)} %constant.56.clone) | copy-start | bytes 49156
  177.4 10.9 %copy-start.4 = (f32[2,96,4096]{1,2,0:T(8,128)S(1)}, f32[2,96,4096]{1,2,0:T(8,128)}, u32[]{:S(2)}) copy-start(f32[2,96,4096]{1,2,0:T(8,128)} %get-tuple-element.19) | copy-start | bytes 9437188
  177.4 10.9 %copy-start.12 = (f32[64,64,1,1]{0,1,3,2:T(8,128)S(1)}, f32[64,64,1,1]{0,1,3,2:T(8,128)}, u32[]{:S(2)}) copy-start(f32[64,64,1,1]{0,1,3,2:T(8,128)} %constant.74) | copy-start | bytes 49156
  188.3 7.1 %copy-start.3 = (f32[2,96,4096]{1,2,0:T(8,128)S(1)}, f32[2,96,4096]{1,2,0:T(8,128)}, u32[]{:S(2)}) copy-start(f32[2,96,4096]{1,2,0:T(8,128)} %get-tuple-element.18) | copy-start | bytes 9437188
  209.7 17.0 %copy-start.11 = (f32[64,64]{0,1:T(8,128)S(1)}, f32[64,64]{0,1:T(8,128)}, u32[]{:S(2)}) copy-start(f32[64,64]{0,1:T(8,128)} %constant.58.clone) | copy-start | bytes 49156
  226.7 6.7 %copy-start = (f32[2,96,64,64]{1,2,3,0:T(8,128)S(1)}, f32[2,96,64,64]{1,2,3,0:T(8,128)}, u32[]{:S(2)}) copy-start(f32[2,96,64,64]{1,2,3,0:T(8,128)} %get-tuple-element.27) | copy-start | bytes 9437188
  233.4 5.6 copy-start.19
  250.8 5.4 copy-start.18
  274.1 3.2 copy-start.27
  284.9 7.8 %copy-start.17 = (f32[134,128,1,1]{1,0,3,2:T(8,128)S(1)}, f32[134,128,1,1]{1,0,3,2:T(8,128)}, u32[]{:S(2)}) copy-start(f32[134,128,1,1]{1,0,3,2:T(8,128)} %constant.80) | copy-start | bytes 205828
  300.9 4.9 copy-start.6
  300.9 5.0 copy-start.14
  312.2 3.4 copy-start.8
  325.3 9.6 %copy-start.23 = (f32[38,32,1,1]{0,1,3,2:T(8,128)S(1)}, f32[38,32,1,1]{0,1,3,2:T(8,128)}, u32[]{:S(2)}) copy-start(f32[38,32,1,1]{0,1,3,2:T(8,128)} %constant.84) | copy-start | bytes 14596
  336.1 4.2 copy-start.24
  (6 other events, 11.5 us)
Sparse Core Ops, SparseCore 0:
  349.1 134.9 all-reduce.1
